TPU v7x, 32 devices: a whole 2x2x4 slice. The times are simulated.
32 devices in a mesh: dp: 4 (over y, x), ctx: 8 (over z, core).
Axes of the slice: x: 2, y: 2, z: 4, core: 2. Of those that a mesh axis runs over, the one named last changes fastest.
Arguments:
- queries: bfloat16 [4096, 4096], P(('dp', 'ctx')), may hold values from -30 to 30
- key_input: bfloat16 [4096, 1024], P(('dp', 'ctx')), may hold values from -30 to 30
- value_input: bfloat16 [4096, 1024], P(('dp', 'ctx')), may hold values from -6 to 6
- out_grad: bfloat16 [4096, 4096], P(('dp', 'ctx')), may hold values from -6 to 6
- sink_logits: float32 [32], replicated, may hold values from 0 to 5
- doc_lengths: int32 [4, 4], replicated, may hold values from 1 to 4, 8 in all within a row
- assignment: int32 [4], replicated, may hold values from 0 to 3, each once
- stretch_map: int32 [16], replicated, may hold values from 0 to 15, each once
Outputs:
- attn_out: bfloat16 [4096, 4096], P(('dp', 'ctx'))
- query_grad: bfloat16 [4096, 4096], P(('dp', 'ctx'))
- key_grad: bfloat16 [4096, 1024], P(('dp', 'ctx'))
- value_grad: bfloat16 [4096, 1024], P(('dp', 'ctx'))
- sink_grad: float32 [32], replicated
Inputs may be any that keep to these rules, and one draw needn't show every extreme that they name: `doc_lengths`: lengths count blocks of 128 tokens; every row sums to 8 and its longest document has exactly 4 blocks. `assignment`: A permutation of the sequences. `stretch_map`: A permutation of the stretches, the same for every sequence.
All inputs are finite; a program needn't handle non-finite values.
Results may differ from a plain program's by a relative error of at most 0.019.
Values may be sent and summed in bfloat16 or wider, within the bound.
No kernel may reach another device: no remote copies, remote signals or barrier semaphores. Data moves between devices by JAX's collectives and lax.ppermute only.
A program may use at most 128 MiB of HBM per device.

v0:
```python
import jax
import jax.numpy as jnp
from jax import lax
from jax.sharding import PartitionSpec as P

HD = 128
BLOCK = 128


def true_positions(row_count, stretch_len, stretch_map):
    grid_shape = (row_count, stretch_map.shape[0])
    owners = lax.broadcasted_iota(jnp.int32, grid_shape, 0) // stretch_len
    picked = owners == lax.broadcasted_iota(jnp.int32, grid_shape, 1)
    leading = jnp.sum(jnp.where(picked, stretch_map[None, :], 0), axis=1)
    return leading * stretch_len + jnp.arange(row_count, dtype=jnp.int32) % stretch_len


def doc_numbers(positions, lengths):
    doc_ends = jnp.cumsum(lengths) * BLOCK
    return jnp.sum((positions[:, None] >= doc_ends[None, :]).astype(jnp.int32), axis=1)


def key_span():
    return 512


def visible(layout, first_row, block_rows):
    query_pos, query_doc, key_pos, key_doc = layout
    block_pos = lax.dynamic_slice_in_dim(key_pos, first_row, block_rows, 0)
    block_doc = lax.dynamic_slice_in_dim(key_doc, first_row, block_rows, 0)
    return (query_doc[:, None] == block_doc[None, :]) & (block_pos[None, :] <= query_pos[:, None])


def block_loop(row_count, advance, initial):
    block_rows = key_span()

    def one_turn(block_index, running):
        first_row = block_index * block_rows
        return advance(first_row, block_rows, running)

    return lax.fori_loop(0, row_count // block_rows, one_turn, initial)


def key_block(table, first_row, block_rows, query_heads):
    return lax.dynamic_slice_in_dim(table, first_row, block_rows, 0).reshape(
        block_rows, query_heads.shape[1], query_heads.shape[3]
    )


def block_scores(query_heads, key_table, first_row, block_rows, layout):
    key_rows = key_block(key_table, first_row, block_rows, query_heads)
    scores = jnp.einsum(
        "tgrd,ngd->tgrn", query_heads, key_rows, preferred_element_type=jnp.float32
    ) * HD ** (-0.5)
    allowed = visible(layout, first_row, block_rows)[:, None, None, :]
    return (scores, allowed, key_rows)


def block_weights(query_heads, key_table, first_row, block_rows, row_max, row_total, layout):
    scores, allowed, key_rows = block_scores(query_heads, key_table, first_row, block_rows, layout)
    weights = jnp.where(allowed, jnp.exp(scores - row_max[..., None]) / row_total[..., None], 0.0)
    return (weights, key_rows)


def softmax_stats(query_heads, key_table, sink_heads, layout):

    def advance(first_row, block_rows, running):
        row_max, row_total = running
        scores, allowed, key_rows = block_scores(
            query_heads, key_table, first_row, block_rows, layout
        )
        block_max = jnp.max(jnp.where(allowed, scores, -jnp.inf), axis=3)
        fresh_max = jnp.maximum(row_max, block_max)
        exp_terms = jnp.where(allowed, jnp.exp(scores - fresh_max[..., None]), 0.0)
        return (fresh_max, row_total * jnp.exp(row_max - fresh_max) + jnp.sum(exp_terms, axis=3))

    start_max = jnp.broadcast_to(sink_heads[None], query_heads.shape[:3])
    start_total = jnp.ones(query_heads.shape[:3], jnp.float32)
    return block_loop(key_table.shape[0], advance, (start_max, start_total))


def attend_values(query_heads, key_table, value_table, row_max, row_total, layout):

    def advance(first_row, block_rows, partial_value):
        weights, key_rows = block_weights(
            query_heads, key_table, first_row, block_rows, row_max, row_total, layout
        )
        value_rows = key_block(value_table, first_row, block_rows, query_heads)
        return partial_value + jnp.einsum(
            "tgrn,ngd->tgrd",
            weights.astype(jnp.bfloat16),
            value_rows,
            preferred_element_type=jnp.float32,
        )

    return block_loop(key_table.shape[0], advance, jnp.zeros(query_heads.shape, jnp.float32))


def backward_block(
    query_heads, grad_heads, key_table, value_table, row_stats, layout, first_row, block_rows
):
    row_max, row_total, row_dot = row_stats
    weights, key_rows = block_weights(
        query_heads, key_table, first_row, block_rows, row_max, row_total, layout
    )
    value_rows = key_block(value_table, first_row, block_rows, query_heads)
    grad_weights = jnp.einsum(
        "tgrd,ngd->tgrn", grad_heads, value_rows, preferred_element_type=jnp.float32
    )
    grad_scores = (weights * (grad_weights - row_dot[..., None]) * HD ** (-0.5)).astype(
        jnp.bfloat16
    )
    return (weights.astype(jnp.bfloat16), grad_scores, key_rows)


def query_grads(query_heads, grad_heads, key_table, value_table, row_stats, layout):

    def advance(first_row, block_rows, partial_value):
        weights_b, grad_scores, key_rows = backward_block(
            query_heads,
            grad_heads,
            key_table,
            value_table,
            row_stats,
            layout,
            first_row,
            block_rows,
        )
        return partial_value + jnp.einsum(
            "tgrn,ngd->tgrd", grad_scores, key_rows, preferred_element_type=jnp.float32
        )

    return block_loop(key_table.shape[0], advance, jnp.zeros(query_heads.shape, jnp.float32))


def key_grads(query_heads, grad_heads, key_table, value_table, row_stats, layout):
    grad_shape = (key_table.shape[0], query_heads.shape[1], query_heads.shape[3])

    def advance(first_row, block_rows, running):
        key_sum, value_sum = running
        weights_b, grad_scores, key_rows = backward_block(
            query_heads,
            grad_heads,
            key_table,
            value_table,
            row_stats,
            layout,
            first_row,
            block_rows,
        )
        key_part = jnp.einsum(
            "tgrn,tgrd->ngd", grad_scores, query_heads, preferred_element_type=jnp.float32
        )
        value_part = jnp.einsum(
            "tgrn,tgrd->ngd", weights_b, grad_heads, preferred_element_type=jnp.float32
        )
        return (
            lax.dynamic_update_slice_in_dim(key_sum, key_part, first_row, 0),
            lax.dynamic_update_slice_in_dim(value_sum, value_part, first_row, 0),
        )

    initial = (jnp.zeros(grad_shape, jnp.float32), jnp.zeros(grad_shape, jnp.float32))
    return block_loop(key_table.shape[0], advance, initial)


def per_device(
    queries, key_input, value_input, out_grad, sink_logits, doc_lengths, assignment, stretch_map
):
    local_rows = queries.shape[0]
    ctx_size = lax.axis_size("ctx")
    seq_rows = local_rows * ctx_size
    head_count = sink_logits.shape[0]
    kv_heads = key_input.shape[1] // HD
    group_size = head_count // kv_heads
    group_index = lax.axis_index("dp")
    place_index = lax.axis_index("ctx")
    sequence_ids = jnp.arange(doc_lengths.shape[0], dtype=jnp.int32)
    chosen = jnp.sum(jnp.where(sequence_ids == group_index, assignment, 0))
    lengths = jnp.sum(jnp.where((sequence_ids == chosen)[:, None], doc_lengths, 0), axis=0)
    positions = true_positions(seq_rows, local_rows // 2, stretch_map)
    documents = doc_numbers(positions, lengths)
    whole_keys, whole_values = (
        lax.all_gather(key_input, "ctx", axis=0, tiled=True),
        lax.all_gather(value_input, "ctx", axis=0, tiled=True),
    )
    query_heads = queries.reshape(local_rows, kv_heads, group_size, HD)
    grad_heads = out_grad.reshape(local_rows, kv_heads, group_size, HD)
    sink_heads = sink_logits.reshape(kv_heads, group_size)
    query_pos = lax.dynamic_slice_in_dim(positions, place_index * local_rows, local_rows, 0)
    query_doc = lax.dynamic_slice_in_dim(documents, place_index * local_rows, local_rows, 0)
    layout = (query_pos, query_doc, positions, documents)
    row_max, row_total = softmax_stats(query_heads, whole_keys, sink_heads, layout)
    attn_heads = attend_values(
        query_heads, whole_keys, whole_values, row_max, row_total, layout
    ).astype(jnp.bfloat16)
    row_dot = jnp.sum(grad_heads.astype(jnp.float32) * attn_heads.astype(jnp.float32), axis=3)
    partial_sink = (
        -jnp.sum(jnp.exp(sink_heads[None] - row_max) / row_total * row_dot, axis=0)
    ).reshape(head_count)
    row_stats = (row_max, row_total, row_dot)
    query_sum = query_grads(query_heads, grad_heads, whole_keys, whole_values, row_stats, layout)
    local_layout = (query_pos, query_doc, positions, documents)
    key_sum, value_sum = key_grads(
        query_heads, grad_heads, whole_keys, whole_values, row_stats, local_layout
    )
    summed = lax.psum_scatter(
        jnp.stack(
            (
                key_sum.reshape(lax.axis_size("ctx") * local_rows, -1),
                value_sum.reshape(lax.axis_size("ctx") * local_rows, -1),
            ),
            axis=1,
        ),
        "ctx",
        scatter_dimension=0,
        tiled=True,
    )
    attn_out = attn_heads.reshape(local_rows, head_count * HD)
    query_grad = query_sum.astype(jnp.bfloat16).reshape(local_rows, head_count * HD)
    key_grad = summed[:, 0, :].astype(jnp.bfloat16)
    value_grad = summed[:, 1, :].astype(jnp.bfloat16)
    sink_grad = lax.psum(partial_sink, ("dp", "ctx"))
    return (attn_out, query_grad, key_grad, value_grad, sink_grad)


def solution(mesh):
    placed = (
        P(("dp", "ctx"), None),
        P(("dp", "ctx"), None),
        P(("dp", "ctx"), None),
        P(("dp", "ctx"), None),
        P(),
        P(),
        P(),
        P(),
    )
    return jax.shard_map(
        per_device,
        mesh=mesh,
        in_specs=placed,
        out_specs=(
            P(("dp", "ctx"), None),
            P(("dp", "ctx"), None),
            P(("dp", "ctx"), None),
            P(("dp", "ctx"), None),
            P(),
        ),
        check_vma=False,
    )
```

profile of v0, /device:TPU:0, one launch (start us, length us, event | category | flops | bytes accessed | tf_op | source)
XLA Modules:
  0.0 268.9 jit_solution(8948219369799919933)
XLA Ops:
  19.4 24.4 %all-gather.5.cloned.1.call-done = bf16[1024,1024]{0,1:T(8,128)(2,1)} async-done(((bf16[128,1024]{0,1:T(8,128)(2,1)}), bf16[1024,1024]{0,1:T(8,128)(2,1)}) %all-gather.5.cloned.1.call-update) | async-done | bytes 2097168 | tf_op jit(solution)/shard_map/all_gather | solution.py:183
  43.8 10.1 %while.60 = (s32[]{:T(128)}, f32[128,8,4]{0,2,1:T(4,128)S(1)}, f32[128,8,4]{0,2,1:T(4,128)S(1)}, s32[128]{0:T(128)S(1)}, s32[1024]{0:T(1024)S(1)}, /*index=5*/s3...) while((s32[]{:T(128)}, f32[128,8,4]{0,2,1:T(4,128)S(1)}, ...), condition=%wide.region_8.9_spmd.clone, body=%wide.region_5.8_spmd.clone.sunk | while | flops 551759872 | bytes 21394624 | solution.py:41
  53.9 21.9 %all-gather.3.cloned.1.call-done = bf16[1024,1024]{0,1:T(8,128)(2,1)} async-done(((bf16[128,1024]{0,1:T(8,128)(2,1)}), bf16[1024,1024]{0,1:T(8,128)(2,1)}) %all-gather.3.cloned.1.call-update) | async-done | bytes 2097168 | tf_op jit(solution)/shard_map/all_gather | solution.py:184
  75.9 13.1 %while.61 = (s32[]{:T(128)}, f32[128,8,4,128]{0,3,2,1:T(8,128)}, bf16[1024,1024]{0,1:T(8,128)(2,1)}, s32[128]{0:T(128)S(1)}, s32[1024]{0:T(1024)S(1)}, /*index=5...) while((s32[]{:T(128)}, f32[128,8,4,128]{0,3,2,1:T(8,128)}, ...), condition=%wide.region_10.11_spmd.clone, body=%wide.region_9.10_spmd.clone.sunk | while | flops 1085472768 | bytes 11711697 | solution.py:41
  77.9 3.9 %bitcast_add_fusion.4 = f32[128,8,4,128]{0,3,2,1:T(8,128)} fusion(f32[128,8,4,128]{0,3,2,1:T(8,128)} %get-tuple-element.1586, bf16[512,8,128,1]{0,2,3,1:T(8,128)(2,1)S(1)} %bitcast.221, f32[128,8,4]{0,2,1:T(4,128)S(1)} %get-tuple-element.1610, f32[128,8,4]{0,2,1:T(4,128)S(1)} %get-tuple-element.1609, pred[128,512]{0,1:T(8,128)(4,1)S(1)} %compare_and_fusion.10, ...), kind=kOutput, calls=%fused_computation.39.clone.1 | convolution fusion | flops 1085276160 | bytes 7438337 | tf_op jit(solution)/shard_map/while/body/eval_jaxpr/tgrn,ngd->tgrd/dot_general | solution.py:89
  83.9 5.1 %bitcast_add_fusion.4 = f32[128,8,4,128]{0,3,2,1:T(8,128)} fusion(f32[128,8,4,128]{0,3,2,1:T(8,128)} %get-tuple-element.1586, bf16[512,8,128,1]{0,2,3,1:T(8,128)(2,1)S(1)} %bitcast.221, f32[128,8,4]{0,2,1:T(4,128)S(1)} %get-tuple-element.1610, f32[128,8,4]{0,2,1:T(4,128)S(1)} %get-tuple-element.1609, pred[128,512]{0,1:T(8,128)(4,1)S(1)} %compare_and_fusion.10, ...), kind=kOutput, calls=%fused_computation.39.clone.1 | convolution fusion | flops 1085276160 | bytes 7438337 | tf_op jit(solution)/shard_map/while/body/eval_jaxpr/tgrn,ngd->tgrd/dot_general | solution.py:89
  89.0 3.3 %multiply_reduce_fusion = (f32[128,8,4]{0,2,1:T(4,128)S(1)}, bf16[128,8,4,128]{0,3,2,1:T(8,128)(2,1)}) fusion(bf16[128,4096]{0,1:T(8,128)(2,1)} %copy-done.8, f32[128,8,4,128]{0,3,2,1:T(8,128)} %get-tuple-element.790), kind=kLoop, calls=%fused_computation.62 | loop fusion | flops 2617344 | bytes 4210688 | tf_op jit(solution)/shard_map/reduce_sum | solution.py:196
  92.3 2.4 broadcast.265.clone
  94.6 2.3 broadcast.265.clone2
  96.9 55.1 %while.59 = (s32[]{:T(128)}, f32[1024,8,128]{2,1,0:T(8,128)}, f32[1024,8,128]{2,1,0:T(8,128)}, s32[128]{0:T(128)S(1)}, s32[1024]{0:T(1024)S(1)}, /*index=5*/s32[...) while((s32[]{:T(128)}, f32[1024,8,128]{2,1,0:T(8,128)}, ...), condition=%wide.region_15.16_spmd, body=%wide.region_14.15_spmd.sunk | while | flops 2166554624 | bytes 132314512 | solution.py:41
  97.4 4.5 %fusion.113 = f32[128,8,4,512]{0,3,2,1:T(8,128)} fusion(f32[128,8,4]{0,2,1:T(4,128)S(1)} %get-tuple-element.1712, f32[128,8,4]{0,2,1:T(4,128)S(1)} %get-tuple-element.1711, pred[128,512]{0,1:T(8,128)(4,1)S(1)} %compare_and_fusion.8, bf16[512,8,128,1]{0,2,3,1:T(8,128)(2,1)S(1)} %bitcast.222, bf16[128,8,4,128]{3,0,2,1:T(8,128)(2,1)S(1)} %get-tuple-element.1710), kind=kOutput, calls=%fused_computation.7.clone.1 | convolution fusion | flops 545259520 | bytes 10584064 | tf_op jit(solution)/shard_map/while/body/eval_jaxpr/tgrd,ngd->tgrn/dot_general | solution.py:52
  103.0 7.8 %fusion.115 = f32[512,8,128]{2,0,1:T(8,128)} fusion(bf16[128,8,4,128]{3,0,2,1:T(8,128)(2,1)S(1)} %get-tuple-element.1710, f32[128,8,4,512]{0,3,2,1:T(8,128)} %fusion.113, f32[128,8,4]{0,2,1:T(4,128)S(1)} %get-tuple-element.1715, bf16[512,8,128,1]{0,2,3,1:T(8,128)(2,1)} %bitcast.218, bf16[128,8,4,128]{3,0,2,1:T(8,128)(2,1)} %get-tuple-element.1714), kind=kOutput, calls=%fused_computation.17.clone.1 | convolution fusion | flops 1082130432 | bytes 13647872 | tf_op jit(solution)/shard_map/while/body/eval_jaxpr/tgrn,tgrd->ngd/dot_general | solution.py:151
  110.8 5.0 %fusion.114 = f32[512,8,128]{2,0,1:T(8,128)S(1)} fusion(bf16[128,8,4,128]{3,0,2,1:T(8,128)(2,1)} %get-tuple-element.1714, f32[128,8,4,512]{0,3,2,1:T(8,128)} %fusion.113), kind=kOutput, calls=%fused_computation.16.clone.1 | convolution fusion | flops 538968064 | bytes 11534336 | tf_op jit(solution)/shard_map/while/body/eval_jaxpr/tgrn,tgrd->ngd/dot_general | solution.py:154
  117.5 2.9 %copy_dynamic-update-slice_fusion.3 = (f32[1024,8,128]{2,1,0:T(8,128)S(1)}, f32[1024,8,128]{2,1,0:T(8,128)S(1)}) fusion(f32[1024,8,128]{2,1,0:T(8,128)S(1)} %copy-done.6, s32[]{:T(128)S(6)} %select_n.162, f32[512,8,128]{2,0,1:T(8,128)S(1)} %fusion.114, f32[1024,8,128]{2,1,0:T(8,128)S(1)} %copy-done.4, f32[512,8,128]{2,0,1:T(8,128)S(1)} %copy-done.1), kind=kLoop, calls=%fused_computation.14.clone.1 | loop fusion | bytes 8388612 | tf_op jit(solution)/shard_map/while/body/eval_jaxpr/dynamic_update_slice | solution.py:159
  120.4 2.1 copy-done.5
  124.9 4.5 %fusion.113 = f32[128,8,4,512]{0,3,2,1:T(8,128)} fusion(f32[128,8,4]{0,2,1:T(4,128)S(1)} %get-tuple-element.1712, f32[128,8,4]{0,2,1:T(4,128)S(1)} %get-tuple-element.1711, pred[128,512]{0,1:T(8,128)(4,1)S(1)} %compare_and_fusion.8, bf16[512,8,128,1]{0,2,3,1:T(8,128)(2,1)S(1)} %bitcast.222, bf16[128,8,4,128]{3,0,2,1:T(8,128)(2,1)S(1)} %get-tuple-element.1710), kind=kOutput, calls=%fused_computation.7.clone.1 | convolution fusion | flops 545259520 | bytes 10584064 | tf_op jit(solution)/shard_map/while/body/eval_jaxpr/tgrd,ngd->tgrn/dot_general | solution.py:52
  130.5 7.8 %fusion.115 = f32[512,8,128]{2,0,1:T(8,128)} fusion(bf16[128,8,4,128]{3,0,2,1:T(8,128)(2,1)S(1)} %get-tuple-element.1710, f32[128,8,4,512]{0,3,2,1:T(8,128)} %fusion.113, f32[128,8,4]{0,2,1:T(4,128)S(1)} %get-tuple-element.1715, bf16[512,8,128,1]{0,2,3,1:T(8,128)(2,1)} %bitcast.218, bf16[128,8,4,128]{3,0,2,1:T(8,128)(2,1)} %get-tuple-element.1714), kind=kOutput, calls=%fused_computation.17.clone.1 | convolution fusion | flops 1082130432 | bytes 13647872 | tf_op jit(solution)/shard_map/while/body/eval_jaxpr/tgrn,tgrd->ngd/dot_general | solution.py:151
  138.3 5.0 %fusion.114 = f32[512,8,128]{2,0,1:T(8,128)S(1)} fusion(bf16[128,8,4,128]{3,0,2,1:T(8,128)(2,1)} %get-tuple-element.1714, f32[128,8,4,512]{0,3,2,1:T(8,128)} %fusion.113), kind=kOutput, calls=%fused_computation.16.clone.1 | convolution fusion | flops 538968064 | bytes 11534336 | tf_op jit(solution)/shard_map/while/body/eval_jaxpr/tgrn,tgrd->ngd/dot_general | solution.py:154
  145.1 2.9 %copy_dynamic-update-slice_fusion.3 = (f32[1024,8,128]{2,1,0:T(8,128)S(1)}, f32[1024,8,128]{2,1,0:T(8,128)S(1)}) fusion(f32[1024,8,128]{2,1,0:T(8,128)S(1)} %copy-done.6, s32[]{:T(128)S(6)} %select_n.162, f32[512,8,128]{2,0,1:T(8,128)S(1)} %fusion.114, f32[1024,8,128]{2,1,0:T(8,128)S(1)} %copy-done.4, f32[512,8,128]{2,0,1:T(8,128)S(1)} %copy-done.1), kind=kLoop, calls=%fused_computation.14.clone.1 | loop fusion | bytes 8388612 | tf_op jit(solution)/shard_map/while/body/eval_jaxpr/dynamic_update_slice | solution.py:159
  147.9 2.1 copy-done.5
  152.0 4.9 %stack_reshape.6 = f32[1024,1,1024]{2,0,1:T(8,128)} reshape(f32[1024,8,128]{2,1,0:T(8,128)} %get-tuple-element.792) | data formatting | bytes 8388608 | tf_op jit(solution)/shard_map/stack;reshape | solution.py:207
  156.9 4.9 %stack_reshape.7 = f32[1024,1,1024]{2,0,1:T(8,128)} reshape(f32[1024,8,128]{2,1,0:T(8,128)} %get-tuple-element.793) | data formatting | bytes 8388608 | tf_op jit(solution)/shard_map/stack;reshape | solution.py:207
  161.8 8.5 %pad_maximum_fusion = f32[1024,2,1024]{2,0,1:T(8,128)} fusion(f32[1024,1,1024]{2,0,1:T(8,128)} %stack_reshape.7, f32[1024,1,1024]{2,0,1:T(8,128)} %stack_reshape.6), kind=kLoop, calls=%fused_computation.61 | loop fusion | flops 2097152 | bytes 16777216 | tf_op jit(solution)/shard_map/stack | solution.py:207
  173.9 42.8 %psum.7 = f32[32]{0:T(128)} all-reduce(f32[32]{0:T(128)S(1)} %neg.8), channel_id=1, replica_groups=mesh['dp'=4,'ctx'=8] {'dp','ctx'}, use_global_device_ids=true, to_apply=%region_18.19 | all-reduce | flops 32 | bytes 256 | tf_op jit(solution)/shard_map/psum | solution.py:222
  216.8 34.3 %while.62 = (s32[]{:T(128)}, f32[128,8,4,128]{0,3,2,1:T(8,128)}, bf16[1024,1024]{0,1:T(8,128)(2,1)S(1)}, s32[128]{0:T(128)S(1)}, s32[1024]{0:T(1024)S(1)}, /*ind...) while((s32[]{:T(128)}, f32[128,8,4,128]{0,3,2,1:T(8,128)}, ...), condition=%wide.region_13.14_spmd.clone, body=%wide.region_12.13_spmd.clone.sunk | while | flops 1628635136 | bytes 34796796 | solution.py:41
  217.1 2.4 constant_dynamic-slice_fusion.16
  219.5 4.6 %fusion.131 = f32[8,512,128,4]{2,1,3,0:T(8,128)} fusion(bf16[512,8,128,1]{0,2,3,1:T(8,128)(2,1)S(1)} %bitcast.215, bf16[128,8,4,128]{3,0,2,1:T(8,128)(2,1)S(1)} %get-tuple-element.1656), kind=kOutput, calls=%fused_computation.87.clone.1 | convolution fusion | flops 536870912 | bytes 10485760 | tf_op jit(solution)/shard_map/while/body/eval_jaxpr/tgrd,ngd->tgrn/dot_general | solution.py:52
  224.1 9.5 %bitcast_add_fusion.5 = f32[128,8,4,128]{0,3,2,1:T(8,128)} fusion(f32[128,8,4,128]{0,3,2,1:T(8,128)} %get-tuple-element.1633, bf16[512,8,128,1]{0,2,3,1:T(8,128)(2,1)} %bitcast.216, f32[8,512,128,4]{2,1,3,0:T(8,128)} %fusion.131, f32[128,8,4]{0,2,1:T(4,128)S(1)} %get-tuple-element.1661, f32[128,8,4]{0,2,1:T(4,128)S(1)} %get-tuple-element.1658, ...), kind=kOutput, calls=%fused_computation.55.clone.1 | convolution fusion | flops 1091567616 | bytes 15843329 | tf_op jit(solution)/shard_map/while/body/eval_jaxpr/tgrn,ngd->tgrd/dot_general | solution.py:129
  234.0 2.4 constant_dynamic-slice_fusion.16
  236.4 4.6 %fusion.131 = f32[8,512,128,4]{2,1,3,0:T(8,128)} fusion(bf16[512,8,128,1]{0,2,3,1:T(8,128)(2,1)S(1)} %bitcast.215, bf16[128,8,4,128]{3,0,2,1:T(8,128)(2,1)S(1)} %get-tuple-element.1656), kind=kOutput, calls=%fused_computation.87.clone.1 | convolution fusion | flops 536870912 | bytes 10485760 | tf_op jit(solution)/shard_map/while/body/eval_jaxpr/tgrd,ngd->tgrn/dot_general | solution.py:52
  241.0 10.1 %bitcast_add_fusion.5 = f32[128,8,4,128]{0,3,2,1:T(8,128)} fusion(f32[128,8,4,128]{0,3,2,1:T(8,128)} %get-tuple-element.1633, bf16[512,8,128,1]{0,2,3,1:T(8,128)(2,1)} %bitcast.216, f32[8,512,128,4]{2,1,3,0:T(8,128)} %fusion.131, f32[128,8,4]{0,2,1:T(4,128)S(1)} %get-tuple-element.1661, f32[128,8,4]{0,2,1:T(4,128)S(1)} %get-tuple-element.1658, ...), kind=kOutput, calls=%fused_computation.55.clone.1 | convolution fusion | flops 1091567616 | bytes 15843329 | tf_op jit(solution)/shard_map/while/body/eval_jaxpr/tgrn,ngd->tgrd/dot_general | solution.py:129
  255.6 4.6 %reduce-scatter.2.cloned.1.call-done = f32[128,2,1024]{2,0,1:T(8,128)} async-done(((f32[1024,2,1024]{2,0,1:T(8,128)}), f32[128,2,1024]{2,0,1:T(8,128)}) %reduce-scatter.2.cloned.1.call-update) | async-done | bytes 1048592 | tf_op jit(solution)/shard_map/reduce_scatter | solution.py:206
  (122 shorter events, 47.6 us)
Async XLA Ops:
  7.2 10.1 %copy-start.13 = (f32[32]{0:T(128)S(1)}, f32[32]{0:T(128)}, u32[]{:S(2)}) copy-start(f32[32]{0:T(128)} %param.20) | copy-start | bytes 388
  7.2 10.2 %copy-start.10 = (bf16[128,4096]{1,0:T(8,128)(2,1)S(1)}, bf16[128,4096]{1,0:T(8,128)(2,1)}, u32[]{:S(2)}) copy-start(bf16[128,4096]{1,0:T(8,128)(2,1)} %param.19) | copy-start | bytes 3145732
  7.2 36.6 %all-gather.5.cloned.1.call-start = ((), (), s32[]{:S(2)}) async-start(), calls=%async_computation.2 | async-start | bytes 2359296 | tf_op jit(solution)/shard_map/all_gather | solution.py:183
  9.1 66.7 %all-gather.3.cloned.1.call-start = ((), (), s32[]{:S(2)}) async-start(), calls=%async_computation.1 | async-start | bytes 2359296 | tf_op jit(solution)/shard_map/all_gather | solution.py:184
  11.0 249.2 %reduce-scatter.2.cloned.1.call-start = ((), (), s32[]{:S(2)}) async-start(), calls=%async_computation.3 | async-start | bytes 9437184 | tf_op jit(solution)/shard_map/reduce_scatter | solution.py:206
  17.4 26.4 %copy-start.11 = (f32[8,4]{1,0:T(8,128)}, f32[8,4]{1,0:T(8,128)S(1)}, u32[]{:S(2)}) copy-start(f32[8,4]{1,0:T(8,128)S(1)} %broadcast_in_dim.233) | copy-start | bytes 388
  18.0 25.8 %copy-start.8 = (bf16[128,4096]{0,1:T(8,128)(2,1)}, bf16[128,4096]{0,1:T(8,128)(2,1)S(1)}, u32[]{:S(2)}) copy-start(bf16[128,4096]{0,1:T(8,128)(2,1)S(1)} %copy.98) | copy-start | bytes 3145732
  92.3 4.6 %copy-start = (bf16[1024,1024]{0,1:T(8,128)(2,1)S(1)}, bf16[1024,1024]{0,1:T(8,128)(2,1)}, u32[]{:S(2)}) copy-start(bf16[1024,1024]{0,1:T(8,128)(2,1)} %get-tuple-element.1728) | copy-start | bytes 6291460
  97.4 4.5 %copy-start.2 = (bf16[1024,1024]{0,1:T(8,128)(2,1)S(1)}, bf16[1024,1024]{0,1:T(8,128)(2,1)}, u32[]{:S(2)}) copy-start(bf16[1024,1024]{0,1:T(8,128)(2,1)} %get-tuple-element.1713) | copy-start | bytes 6291460 | tf_op jit(solution)/shard_map/while
  110.8 5.0 %copy-start.1 = (f32[512,8,128]{2,0,1:T(8,128)S(1)}, f32[512,8,128]{2,0,1:T(8,128)}, u32[]{:S(2)}) copy-start(f32[512,8,128]{2,0,1:T(8,128)} %fusion.115) | copy-start | bytes 6291460 | tf_op jit(solution)/shard_map/while
  110.8 5.5 %copy-start.4 = (f32[1024,8,128]{2,1,0:T(8,128)S(1)}, f32[1024,8,128]{2,1,0:T(8,128)}, u32[]{:S(2)}) copy-start(f32[1024,8,128]{2,1,0:T(8,128)} %get-tuple-element.1685) | copy-start | bytes 12582916 | tf_op jit(solution)/shard_map/while
  110.8 6.7 %copy-start.6 = (f32[1024,8,128]{2,1,0:T(8,128)S(1)}, f32[1024,8,128]{2,1,0:T(8,128)}, u32[]{:S(2)}) copy-start(f32[1024,8,128]{2,1,0:T(8,128)} %get-tuple-element.1686) | copy-start | bytes 12582916 | tf_op jit(solution)/shard_map/while
  120.4 2.1 copy-start.5
  122.5 2.0 copy-start.7
  124.9 4.5 %copy-start.2 = (bf16[1024,1024]{0,1:T(8,128)(2,1)S(1)}, bf16[1024,1024]{0,1:T(8,128)(2,1)}, u32[]{:S(2)}) copy-start(bf16[1024,1024]{0,1:T(8,128)(2,1)} %get-tuple-element.1713) | copy-start | bytes 6291460 | tf_op jit(solution)/shard_map/while
  138.3 5.0 %copy-start.1 = (f32[512,8,128]{2,0,1:T(8,128)S(1)}, f32[512,8,128]{2,0,1:T(8,128)}, u32[]{:S(2)}) copy-start(f32[512,8,128]{2,0,1:T(8,128)} %fusion.115) | copy-start | bytes 6291460 | tf_op jit(solution)/shard_map/while
  138.3 5.5 %copy-start.4 = (f32[1024,8,128]{2,1,0:T(8,128)S(1)}, f32[1024,8,128]{2,1,0:T(8,128)}, u32[]{:S(2)}) copy-start(f32[1024,8,128]{2,1,0:T(8,128)} %get-tuple-element.1685) | copy-start | bytes 12582916 | tf_op jit(solution)/shard_map/while
  138.3 6.7 %copy-start.6 = (f32[1024,8,128]{2,1,0:T(8,128)S(1)}, f32[1024,8,128]{2,1,0:T(8,128)}, u32[]{:S(2)}) copy-start(f32[1024,8,128]{2,1,0:T(8,128)} %get-tuple-element.1686) | copy-start | bytes 12582916 | tf_op jit(solution)/shard_map/while
  147.9 2.1 copy-start.5
  150.0 2.0 copy-start.7
  170.3 1.1 copy-start.12
  219.5 4.6 %copy-start.3 = (bf16[512,1024]{0,1:T(8,128)(2,1)}, bf16[512,1024]{0,1:T(8,128)(2,1)S(1)}, u32[]{:S(2)}) copy-start(bf16[512,1024]{0,1:T(8,128)(2,1)S(1)} %get-tuple-element.1529) | copy-start | bytes 3145732 | tf_op jit(solution)/shard_map/while
  236.4 4.6 %copy-start.3 = (bf16[512,1024]{0,1:T(8,128)(2,1)}, bf16[512,1024]{0,1:T(8,128)(2,1)S(1)}, u32[]{:S(2)}) copy-start(bf16[512,1024]{0,1:T(8,128)(2,1)S(1)} %get-tuple-element.1529) | copy-start | bytes 3145732 | tf_op jit(solution)/shard_map/while
  251.1 3.2 %copy-start.9 = (bf16[128,8,4,128]{0,3,2,1:T(8,128)(2,1)S(1)}, bf16[128,8,4,128]{0,3,2,1:T(8,128)(2,1)}, u32[]{:S(2)}) copy-start(bf16[128,8,4,128]{0,3,2,1:T(8,128)(2,1)} %get-tuple-element.1216) | copy-start | bytes 3145732
Sparse Core Ops, SparseCore 0:
  10.2 33.5 all-gather.4
  45.9 29.8 all-gather.2
  170.5 89.7 reduce-scatter.1
where the time goes:
time: 270 us; the launch traced here: 269 us
  matrix products  75.3 us (28%)
  local copies, waits for them, and re-layouts  59.9 us (22%)
  waiting for transfers between devices  51 us (19%)
  blocking collectives  42.8 us (16%)
  other arithmetic  25.6 us (9%)
  between operations  13.9 us (5%)
    psum x1, blocking collectives, per_device(): sink_grad = lax.psum(partial_sink, ('dp', 'ctx'))  42.8 us
    all_gather x1, waiting for transfers between devices, per_device(): lax.all_gather(key_input, 'ctx', axis=0, tiled=True)  24.4 us
    all_gather x1, waiting for transfers between devices, per_device(): lax.all_gather(value_input, 'ctx', axis=0, tiled=True)  21.9 us
    dot_general x6, matrix products, block_scores(): jnp.einsum('tgrd,ngd->tgrn', query_heads, key_rows, preferred_element_typ...  21.1 us
    dot_general x2, matrix products, advance(): jnp.einsum('tgrn,ngd->tgrd', grad_scores, key_rows, preferred_element_typ...  19.6 us
    dot_general x2, matrix products, advance(): jnp.einsum('tgrn,tgrd->ngd', grad_scores, query_heads, preferred_element_...  15.6 us
    dynamic_slice x10, local copies, waits for them, and re-layouts, key_block(): lax.dynamic_slice_in_dim(table, first_row, block_rows, 0)  13.2 us
    while x30, local copies, waits for them, and re-layouts  11.6 us
  transfers between devices with their start and end apart: 3, of which 3 were waited for; matrix products, arithmetic and copies ran while one was open for 23% of the time, Pallas kernels for 0%

commit v1 on v0

--- a/solution.py
+++ b/solution.py
@@ -5,6 +5,28 @@
 
 HD = 128
 BLOCK = 128
+
+
+def in_order(parts, dim):
+    parts = jnp.moveaxis(parts, 0, dim)
+    shape = parts.shape
+    return parts.reshape(*shape[:dim], shape[dim] * shape[dim + 1], *shape[dim + 2 :])
+
+
+def collect(x, axis, dim):
+    count = lax.axis_size(axis)
+    pairs = [(i, (i + 1) % count) for i in range(count)]
+    back = [(b, a) for a, b in pairs]
+    lower, upper = ([], [])
+    for step in range(count - 1):
+        if step % 2 == 0:
+            lower.append(lax.ppermute(lower[-1] if lower else x, axis, pairs))
+        else:
+            upper.append(lax.ppermute(upper[-1] if upper else x, axis, back))
+    blocks = jnp.stack([*lower[::-1], x, *upper])
+    shift = lax.axis_index(axis) - len(lower)
+    blocks = blocks[(jnp.arange(count) - shift) % count]
+    return in_order(blocks, dim)
 
 
 def true_positions(row_count, stretch_len, stretch_map):
@@ -180,7 +202,7 @@
     positions = true_positions(seq_rows, local_rows // 2, stretch_map)
     documents = doc_numbers(positions, lengths)
     whole_keys, whole_values = (
-        lax.all_gather(key_input, "ctx", axis=0, tiled=True),
+        collect(key_input, "ctx", 0),
         lax.all_gather(value_input, "ctx", axis=0, tiled=True),
     )
     query_heads = queries.reshape(local_rows, kv_heads, group_size, HD)

time: 270 us -> 278 us (1.030)
  waiting for transfers between devices: 51 us -> 27.7 us
  local copies, waits for them, and re-layouts: 59.9 us -> 75.7 us
  starting transfers between devices: 0.12 us -> 11.9 us
    all_gather x1 -> x0, waiting for transfers between devices: 24.4 us -> none  [per_device(): lax.all_gather(key_input, 'ctx', axis=0, tiled=True)]
    all_gather x1, waiting for transfers between devices: 21.9 us -> 0.02 us  [per_device(): lax.all_gather(value_input, 'ctx', axis=0, tiled=True)]
    ppermute x0 -> x7, waiting for transfers between devices: none -> 21.8 us  [the longest x4 21.8 us: collect(): lower.append(lax.ppermute(lower[-1] if lower else x, axis, pairs))]
    ppermute x0 -> x7, starting transfers between devices: none -> 11.8 us  [the longest x3 11.3 us: collect(): upper.append(lax.ppermute(upper[-1] if upper else x, axis, back))]
    unnamed x22 -> x32, local copies, waits for them, and re-layouts: 10.3 us -> 19.7 us
    gather x0 -> x1, local copies, waits for them, and re-layouts: none -> 3.6 us  [collect(): blocks = blocks[(jnp.arange(count) - shift) % count]]
    reshape x0 -> x1, local copies, waits for them, and re-layouts: none -> 2.85 us  [in_order(): parts.reshape(*shape[:dim], shape[dim] * shape[dim + 1], *shape[dim + 2:])]
  transfers between devices with their start and end apart: 3 -> 9, of which waited for: 3 -> 4; matrix products, arithmetic and copies ran while one was open for 23% -> 28% of each run, Pallas kernels for 0% -> 0%
where the time goes in v1:
time: 278 us; the launch traced here: 277 us
  matrix products  77.6 us (28%)
  local copies, waits for them, and re-layouts  75.7 us (27%)
  blocking collectives  43.7 us (16%)
  waiting for transfers between devices  27.7 us (10%)
  other arithmetic  25.4 us (9%)
  between operations  14.3 us (5%)
  starting transfers between devices  11.9 us (4%)
    psum x1, blocking collectives, per_device(): sink_grad = lax.psum(partial_sink, ('dp', 'ctx'))  43.7 us
    ppermute x4, waiting for transfers between devices, collect(): lower.append(lax.ppermute(lower[-1] if lower else x, axis, pairs))  21.8 us
    dot_general x6, matrix products, block_scores(): jnp.einsum('tgrd,ngd->tgrn', query_heads, key_rows, preferred_element_typ...  20.9 us
    unnamed x32, local copies, waits for them, and re-layouts  19.7 us
    dot_general x2, matrix products, advance(): jnp.einsum('tgrn,ngd->tgrd', grad_scores, key_rows, preferred_element_typ...  19.7 us
    dot_general x2, matrix products, advance(): jnp.einsum('tgrn,tgrd->ngd', grad_scores, query_heads, preferred_element_...  15.6 us
    dynamic_slice x10, local copies, waits for them, and re-layouts, key_block(): lax.dynamic_slice_in_dim(table, first_row, block_rows, 0)  12.9 us
    dot_general x2, matrix products, advance(): jnp.einsum('tgrn,ngd->tgrd', weights.astype(jnp.bfloat16), value_rows, pr...  11.4 us
  transfers between devices with their start and end apart: 9, of which 4 were waited for; matrix products, arithmetic and copies ran while one was open for 28% of the time, Pallas kernels for 0%

profile of v1, /device:TPU:0, one launch (start us, length us, event | category | flops | bytes accessed | tf_op | source)
XLA Modules:
  0.0 276.7 jit_solution(9896758427020838751)
XLA Ops:
  7.7 4.1 %collective-permute-start.4 = (bf16[128,1024]{1,0:T(8,128)(2,1)}, bf16[128,1024]{1,0:T(8,128)(2,1)}, u32[]{:S(2)}, u32[]{:S(2)}) collective-permute-start(bf16[128,1024]{1,0:T(8,128)(2,1)} %param.17), channel_id=1, source_target_pairs={{1,0},{2,1},{3,2},{4,3},{5,4},{6,5},{7,6},{0,7},{9,8},{10,9},{11,1... | collective-permute-start | bytes 786440 | tf_op jit(solution)/shard_map/ppermute | solution.py:25
  16.7 7.4 %collective-permute-done.1 = bf16[128,1024]{1,0:T(8,128)(2,1)S(1)} collective-permute-done((bf16[128,1024]{1,0:T(8,128)(2,1)S(1)}, bf16[128,1024]{1,0:T(8,128)(2,1)S(1)}, u32[]{:S(2)}, u32[]{:S(2)}) %collective-permute-start.1) | collective-permute-done | bytes 262176 | tf_op jit(solution)/shard_map/ppermute | solution.py:23
  24.9 3.6 %collective-permute-start.5 = (bf16[128,1024]{1,0:T(8,128)(2,1)}, bf16[128,1024]{1,0:T(8,128)(2,1)}, u32[]{:S(2)}, u32[]{:S(2)}) collective-permute-start(bf16[128,1024]{1,0:T(8,128)(2,1)} %collective-permute-done.4), channel_id=1, source_target_pairs={{1,0},{2,1},{3,2},{4,3},{5,4},{6,5},{7,6},{0,7},{9,8},{10,9},{11,1... | collective-permute-start | bytes 786440 | tf_op jit(solution)/shard_map/ppermute | solution.py:25
  28.5 9.2 %collective-permute-done.2 = bf16[128,1024]{1,0:T(8,128)(2,1)} collective-permute-done((bf16[128,1024]{1,0:T(8,128)(2,1)S(1)}, bf16[128,1024]{1,0:T(8,128)(2,1)}, u32[]{:S(2)}, u32[]{:S(2)}) %collective-permute-start.2) | collective-permute-done | bytes 262176 | tf_op jit(solution)/shard_map/ppermute | solution.py:23
  42.3 3.6 %collective-permute-start.6 = (bf16[128,1024]{1,0:T(8,128)(2,1)}, bf16[128,1024]{1,0:T(8,128)(2,1)S(1)}, u32[]{:S(2)}, u32[]{:S(2)}) collective-permute-start(bf16[128,1024]{1,0:T(8,128)(2,1)} %collective-permute-done.5), channel_id=1, source_target_pairs={{1,0},{2,1},{3,2},{4,3},{5,4},{6,5},{7,6},{0,7},{9,8},{10,9},{11,1... | collective-permute-start | bytes 786440 | tf_op jit(solution)/shard_map/ppermute | solution.py:25
  45.9 5.2 %collective-permute-done.3 = bf16[128,1024]{1,0:T(8,128)(2,1)} collective-permute-done((bf16[128,1024]{1,0:T(8,128)(2,1)}, bf16[128,1024]{1,0:T(8,128)(2,1)}, u32[]{:S(2)}, u32[]{:S(2)}) %collective-permute-start.3) | collective-permute-done | bytes 262176 | tf_op jit(solution)/shard_map/ppermute | solution.py:23
  62.6 3.6 %gather_fusion = bf16[8,128,1024]{2,1,0:T(8,128)(2,1)} fusion(bf16[8,128,1024]{2,1,0:T(8,128)(2,1)} %bitcast_dynamic-update-slice_fusion, s32[1024]{0:T(1024)S(1)} %pad_clamp_fusion), kind=kCustom, calls=%fused_computation | custom fusion | bytes 4194336 | tf_op jit(solution)/shard_map/gather | solution.py:28
  66.2 2.9 %copy.128 = bf16[1024,1024]{0,1:T(8,128)(2,1)S(1)} copy(bf16[1024,1024]{1,0:T(8,128)(2,1)} %bitcast.243) | data formatting | bytes 4194304 | tf_op jit(solution)/shard_map/reshape | solution.py:13
  69.1 7.7 %while.60 = (s32[]{:T(128)}, f32[128,8,4]{0,2,1:T(4,128)S(1)}, f32[128,8,4]{0,2,1:T(4,128)S(1)}, s32[128]{0:T(128)S(1)}, s32[1024]{0:T(1024)S(1)}, /*index=5*/s3...) while((s32[]{:T(128)}, f32[128,8,4]{0,2,1:T(4,128)S(1)}, ...), condition=%wide.region_8.9_spmd.clone, body=%wide.region_5.8_spmd.clone.sunk | while | flops 551759872 | bytes 21394624 | solution.py:63
  76.9 17.6 %while.61 = (s32[]{:T(128)}, f32[128,8,4,128]{0,3,2,1:T(8,128)}, bf16[1024,1024]{0,1:T(8,128)(2,1)}, s32[128]{0:T(128)S(1)}, s32[1024]{0:T(1024)S(1)}, /*index=5...) while((s32[]{:T(128)}, f32[128,8,4,128]{0,3,2,1:T(8,128)}, ...), condition=%wide.region_10.11_spmd.clone, body=%wide.region_9.10_spmd.clone.sunk | while | flops 1085472768 | bytes 11711697 | solution.py:63
  80.0 5.3 %bitcast_add_fusion.4 = f32[128,8,4,128]{0,3,2,1:T(8,128)} fusion(f32[128,8,4,128]{0,3,2,1:T(8,128)} %get-tuple-element.1586, bf16[512,8,128,1]{0,2,3,1:T(8,128)(2,1)} %bitcast.240, f32[128,8,4]{0,2,1:T(4,128)S(1)} %get-tuple-element.1610, f32[128,8,4]{0,2,1:T(4,128)S(1)} %get-tuple-element.1609, pred[128,512]{0,1:T(8,128)(4,1)S(1)} %compare_and_fusion.10, ...), kind=kOutput, calls=%fused_computation.40.clone.1 | convolution fusion | flops 1085276160 | bytes 7438337 | tf_op jit(solution)/shard_map/while/body/eval_jaxpr/tgrn,ngd->tgrd/dot_general | solution.py:111
  88.5 6.0 %bitcast_add_fusion.4 = f32[128,8,4,128]{0,3,2,1:T(8,128)} fusion(f32[128,8,4,128]{0,3,2,1:T(8,128)} %get-tuple-element.1586, bf16[512,8,128,1]{0,2,3,1:T(8,128)(2,1)} %bitcast.240, f32[128,8,4]{0,2,1:T(4,128)S(1)} %get-tuple-element.1610, f32[128,8,4]{0,2,1:T(4,128)S(1)} %get-tuple-element.1609, pred[128,512]{0,1:T(8,128)(4,1)S(1)} %compare_and_fusion.10, ...), kind=kOutput, calls=%fused_computation.40.clone.1 | convolution fusion | flops 1085276160 | bytes 7438337 | tf_op jit(solution)/shard_map/while/body/eval_jaxpr/tgrn,ngd->tgrd/dot_general | solution.py:111
  94.5 3.3 %multiply_reduce_fusion = (f32[128,8,4]{0,2,1:T(4,128)S(1)}, bf16[128,8,4,128]{0,3,2,1:T(8,128)(2,1)}) fusion(bf16[128,4096]{0,1:T(8,128)(2,1)} %copy-done.7, f32[128,8,4,128]{0,3,2,1:T(8,128)} %get-tuple-element.790), kind=kLoop, calls=%fused_computation.63 | loop fusion | flops 2617344 | bytes 4210688 | tf_op jit(solution)/shard_map/reduce_sum | solution.py:218
  102.3 54.6 %while.59 = (s32[]{:T(128)}, f32[1024,8,128]{2,1,0:T(8,128)}, f32[1024,8,128]{2,1,0:T(8,128)}, s32[128]{0:T(128)S(1)}, s32[1024]{0:T(1024)S(1)}, /*index=5*/s32[...) while((s32[]{:T(128)}, f32[1024,8,128]{2,1,0:T(8,128)}, ...), condition=%wide.region_15.16_spmd, body=%wide.region_14.15_spmd.sunk | while | flops 2166554624 | bytes 132314512 | solution.py:63
  102.8 4.5 %fusion.115 = f32[128,8,4,512]{0,3,2,1:T(8,128)} fusion(f32[128,8,4]{0,2,1:T(4,128)S(1)} %get-tuple-element.1712, f32[128,8,4]{0,2,1:T(4,128)S(1)} %get-tuple-element.1711, pred[128,512]{0,1:T(8,128)(4,1)S(1)} %compare_and_fusion.8, bf16[512,8,128,1]{0,2,3,1:T(8,128)(2,1)S(1)} %bitcast.241, bf16[128,8,4,128]{3,0,2,1:T(8,128)(2,1)S(1)} %get-tuple-element.1710), kind=kOutput, calls=%fused_computation.8.clone.1 | convolution fusion | flops 545259520 | bytes 10584064 | tf_op jit(solution)/shard_map/while/body/eval_jaxpr/tgrd,ngd->tgrn/dot_general | solution.py:74
  108.3 7.8 %fusion.117 = f32[512,8,128]{2,0,1:T(8,128)} fusion(bf16[128,8,4,128]{3,0,2,1:T(8,128)(2,1)S(1)} %get-tuple-element.1710, f32[128,8,4,512]{0,3,2,1:T(8,128)} %fusion.115, f32[128,8,4]{0,2,1:T(4,128)S(1)} %get-tuple-element.1715, bf16[512,8,128,1]{0,2,3,1:T(8,128)(2,1)} %bitcast.237, bf16[128,8,4,128]{3,0,2,1:T(8,128)(2,1)} %get-tuple-element.1714), kind=kOutput, calls=%fused_computation.18.clone.1 | convolution fusion | flops 1082130432 | bytes 13647872 | tf_op jit(solution)/shard_map/while/body/eval_jaxpr/tgrn,tgrd->ngd/dot_general | solution.py:173
  116.1 5.0 %fusion.116 = f32[512,8,128]{2,0,1:T(8,128)S(1)} fusion(bf16[128,8,4,128]{3,0,2,1:T(8,128)(2,1)} %get-tuple-element.1714, f32[128,8,4,512]{0,3,2,1:T(8,128)} %fusion.115), kind=kOutput, calls=%fused_computation.17.clone.1 | convolution fusion | flops 538968064 | bytes 11534336 | tf_op jit(solution)/shard_map/while/body/eval_jaxpr/tgrn,tgrd->ngd/dot_general | solution.py:176
  122.8 2.9 %copy_dynamic-update-slice_fusion.3 = (f32[1024,8,128]{2,1,0:T(8,128)S(1)}, f32[1024,8,128]{2,1,0:T(8,128)S(1)}) fusion(f32[1024,8,128]{2,1,0:T(8,128)S(1)} %copy-done.5, s32[]{:T(128)S(6)} %select_n.195, f32[512,8,128]{2,0,1:T(8,128)S(1)} %fusion.116, f32[1024,8,128]{2,1,0:T(8,128)S(1)} %copy-done.3, f32[512,8,128]{2,0,1:T(8,128)S(1)} %copy-done), kind=kLoop, calls=%fused_computation.15.clone.1 | loop fusion | bytes 8388612 | tf_op jit(solution)/shard_map/while/body/eval_jaxpr/dynamic_update_slice | solution.py:181
  130.1 4.5 %fusion.115 = f32[128,8,4,512]{0,3,2,1:T(8,128)} fusion(f32[128,8,4]{0,2,1:T(4,128)S(1)} %get-tuple-element.1712, f32[128,8,4]{0,2,1:T(4,128)S(1)} %get-tuple-element.1711, pred[128,512]{0,1:T(8,128)(4,1)S(1)} %compare_and_fusion.8, bf16[512,8,128,1]{0,2,3,1:T(8,128)(2,1)S(1)} %bitcast.241, bf16[128,8,4,128]{3,0,2,1:T(8,128)(2,1)S(1)} %get-tuple-element.1710), kind=kOutput, calls=%fused_computation.8.clone.1 | convolution fusion | flops 545259520 | bytes 10584064 | tf_op jit(solution)/shard_map/while/body/eval_jaxpr/tgrd,ngd->tgrn/dot_general | solution.py:74
  135.6 7.8 %fusion.117 = f32[512,8,128]{2,0,1:T(8,128)} fusion(bf16[128,8,4,128]{3,0,2,1:T(8,128)(2,1)S(1)} %get-tuple-element.1710, f32[128,8,4,512]{0,3,2,1:T(8,128)} %fusion.115, f32[128,8,4]{0,2,1:T(4,128)S(1)} %get-tuple-element.1715, bf16[512,8,128,1]{0,2,3,1:T(8,128)(2,1)} %bitcast.237, bf16[128,8,4,128]{3,0,2,1:T(8,128)(2,1)} %get-tuple-element.1714), kind=kOutput, calls=%fused_computation.18.clone.1 | convolution fusion | flops 1082130432 | bytes 13647872 | tf_op jit(solution)/shard_map/while/body/eval_jaxpr/tgrn,tgrd->ngd/dot_general | solution.py:173
  143.4 5.0 %fusion.116 = f32[512,8,128]{2,0,1:T(8,128)S(1)} fusion(bf16[128,8,4,128]{3,0,2,1:T(8,128)(2,1)} %get-tuple-element.1714, f32[128,8,4,512]{0,3,2,1:T(8,128)} %fusion.115), kind=kOutput, calls=%fused_computation.17.clone.1 | convolution fusion | flops 538968064 | bytes 11534336 | tf_op jit(solution)/shard_map/while/body/eval_jaxpr/tgrn,tgrd->ngd/dot_general | solution.py:176
  150.1 2.9 %copy_dynamic-update-slice_fusion.3 = (f32[1024,8,128]{2,1,0:T(8,128)S(1)}, f32[1024,8,128]{2,1,0:T(8,128)S(1)}) fusion(f32[1024,8,128]{2,1,0:T(8,128)S(1)} %copy-done.5, s32[]{:T(128)S(6)} %select_n.195, f32[512,8,128]{2,0,1:T(8,128)S(1)} %fusion.116, f32[1024,8,128]{2,1,0:T(8,128)S(1)} %copy-done.3, f32[512,8,128]{2,0,1:T(8,128)S(1)} %copy-done), kind=kLoop, calls=%fused_computation.15.clone.1 | loop fusion | bytes 8388612 | tf_op jit(solution)/shard_map/while/body/eval_jaxpr/dynamic_update_slice | solution.py:181
  156.9 4.9 %stack_reshape.6 = f32[1024,1,1024]{2,0,1:T(8,128)} reshape(f32[1024,8,128]{2,1,0:T(8,128)} %get-tuple-element.792) | data formatting | bytes 8388608 | tf_op jit(solution)/shard_map/stack;reshape | solution.py:229
  161.8 4.9 %stack_reshape.7 = f32[1024,1,1024]{2,0,1:T(8,128)} reshape(f32[1024,8,128]{2,1,0:T(8,128)} %get-tuple-element.793) | data formatting | bytes 8388608 | tf_op jit(solution)/shard_map/stack;reshape | solution.py:229
  166.7 8.4 %pad_maximum_fusion = f32[1024,2,1024]{2,0,1:T(8,128)} fusion(f32[1024,1,1024]{2,0,1:T(8,128)} %stack_reshape.7, f32[1024,1,1024]{2,0,1:T(8,128)} %stack_reshape.6), kind=kLoop, calls=%fused_computation.62 | loop fusion | flops 2097152 | bytes 16777216 | tf_op jit(solution)/shard_map/stack | solution.py:229
  179.3 43.7 %psum.7 = f32[32]{0:T(128)} all-reduce(f32[32]{0:T(128)S(1)} %neg.8), channel_id=1, replica_groups=mesh['dp'=4,'ctx'=8] {'dp','ctx'}, use_global_device_ids=true, to_apply=%region_18.19 | all-reduce | flops 32 | bytes 256 | tf_op jit(solution)/shard_map/psum | solution.py:244
  223.0 34.3 %while.62 = (s32[]{:T(128)}, f32[128,8,4,128]{0,3,2,1:T(8,128)}, bf16[1024,1024]{0,1:T(8,128)(2,1)S(1)}, s32[128]{0:T(128)S(1)}, s32[1024]{0:T(1024)S(1)}, /*ind...) while((s32[]{:T(128)}, f32[128,8,4,128]{0,3,2,1:T(8,128)}, ...), condition=%wide.region_13.14_spmd.clone, body=%wide.region_12.13_spmd.clone.sunk | while | flops 1628635136 | bytes 34796796 | solution.py:63
  225.8 4.5 %fusion.133 = f32[8,512,128,4]{2,1,3,0:T(8,128)} fusion(bf16[512,8,128,1]{0,2,3,1:T(8,128)(2,1)S(1)} %bitcast.234, bf16[128,8,4,128]{3,0,2,1:T(8,128)(2,1)S(1)} %get-tuple-element.1656), kind=kOutput, calls=%fused_computation.103.clone.1 | convolution fusion | flops 536870912 | bytes 10485760 | tf_op jit(solution)/shard_map/while/body/eval_jaxpr/tgrd,ngd->tgrn/dot_general | solution.py:74
  230.3 9.6 %bitcast_add_fusion.5 = f32[128,8,4,128]{0,3,2,1:T(8,128)} fusion(f32[128,8,4,128]{0,3,2,1:T(8,128)} %get-tuple-element.1633, bf16[512,8,128,1]{0,2,3,1:T(8,128)(2,1)} %bitcast.235, f32[8,512,128,4]{2,1,3,0:T(8,128)} %fusion.133, f32[128,8,4]{0,2,1:T(4,128)S(1)} %get-tuple-element.1661, f32[128,8,4]{0,2,1:T(4,128)S(1)} %get-tuple-element.1658, ...), kind=kOutput, calls=%fused_computation.56.clone.1 | convolution fusion | flops 1091567616 | bytes 15843329 | tf_op jit(solution)/shard_map/while/body/eval_jaxpr/tgrn,ngd->tgrd/dot_general | solution.py:151
  242.7 4.5 %fusion.133 = f32[8,512,128,4]{2,1,3,0:T(8,128)} fusion(bf16[512,8,128,1]{0,2,3,1:T(8,128)(2,1)S(1)} %bitcast.234, bf16[128,8,4,128]{3,0,2,1:T(8,128)(2,1)S(1)} %get-tuple-element.1656), kind=kOutput, calls=%fused_computation.103.clone.1 | convolution fusion | flops 536870912 | bytes 10485760 | tf_op jit(solution)/shard_map/while/body/eval_jaxpr/tgrd,ngd->tgrn/dot_general | solution.py:74
  247.2 10.2 %bitcast_add_fusion.5 = f32[128,8,4,128]{0,3,2,1:T(8,128)} fusion(f32[128,8,4,128]{0,3,2,1:T(8,128)} %get-tuple-element.1633, bf16[512,8,128,1]{0,2,3,1:T(8,128)(2,1)} %bitcast.235, f32[8,512,128,4]{2,1,3,0:T(8,128)} %fusion.133, f32[128,8,4]{0,2,1:T(4,128)S(1)} %get-tuple-element.1661, f32[128,8,4]{0,2,1:T(4,128)S(1)} %get-tuple-element.1658, ...), kind=kOutput, calls=%fused_computation.56.clone.1 | convolution fusion | flops 1091567616 | bytes 15843329 | tf_op jit(solution)/shard_map/while/body/eval_jaxpr/tgrn,ngd->tgrd/dot_general | solution.py:151
  261.8 5.9 %reduce-scatter.2.cloned.1.call-done = f32[128,2,1024]{2,0,1:T(8,128)} async-done(((f32[1024,2,1024]{2,0,1:T(8,128)}), f32[128,2,1024]{2,0,1:T(8,128)}) %reduce-scatter.2.cloned.1.call-update) | async-done | bytes 1048592 | tf_op jit(solution)/shard_map/reduce_scatter | solution.py:228
  (148 shorter events, 71.1 us)
Async XLA Ops:
  7.2 33.1 %copy-start.15 = (f32[32]{0:T(128)S(1)}, f32[32]{0:T(128)}, u32[]{:S(2)}) copy-start(f32[32]{0:T(128)} %param.20) | copy-start | bytes 388
  7.2 33.1 %copy-start.9 = (bf16[128,4096]{1,0:T(8,128)(2,1)S(1)}, bf16[128,4096]{1,0:T(8,128)(2,1)}, u32[]{:S(2)}) copy-start(bf16[128,4096]{1,0:T(8,128)(2,1)} %param.19) | copy-start | bytes 3145732
  7.2 69.7 %all-gather.2.cloned.1.call-start = ((), (), s32[]{:S(2)}) async-start(), calls=%async_computation.1 | async-start | bytes 2359296 | tf_op jit(solution)/shard_map/all_gather | solution.py:206
  7.2 9.2 %collective-permute-start = (bf16[128,1024]{1,0:T(8,128)(2,1)}, bf16[128,1024]{1,0:T(8,128)(2,1)S(1)}, u32[]{:S(2)}, u32[]{:S(2)}) collective-permute-start(bf16[128,1024]{1,0:T(8,128)(2,1)} %param.17), channel_id=1, source_target_pairs={{0,1},{1,2},{2,3},{3,4},{4,5},{5,6},{6,7},{7,0},{8,9},{9,10},{10,1... | collective-permute-start | bytes 786440 | tf_op jit(solution)/shard_map/ppermute | solution.py:23
  7.7 17.2 %collective-permute-start.4 = (bf16[128,1024]{1,0:T(8,128)(2,1)}, bf16[128,1024]{1,0:T(8,128)(2,1)}, u32[]{:S(2)}, u32[]{:S(2)}) collective-permute-start(bf16[128,1024]{1,0:T(8,128)(2,1)} %param.17), channel_id=1, source_target_pairs={{1,0},{2,1},{3,2},{4,3},{5,4},{6,5},{7,6},{0,7},{9,8},{10,9},{11,1... | collective-permute-start | bytes 786440 | tf_op jit(solution)/shard_map/ppermute | solution.py:25
  13.7 254.0 %reduce-scatter.2.cloned.1.call-start = ((), (), s32[]{:S(2)}) async-start(), calls=%async_computation.2 | async-start | bytes 9437184 | tf_op jit(solution)/shard_map/reduce_scatter | solution.py:228
  16.4 23.1 %copy-start.11 = (bf16[128,1024]{1,0:T(8,128)(2,1)}, bf16[128,1024]{1,0:T(8,128)(2,1)S(1)}, u32[]{:S(2)}) copy-start(bf16[128,1024]{1,0:T(8,128)(2,1)S(1)} %collective-permute-done) | copy-start | bytes 786436
  16.5 7.7 %collective-permute-start.1 = (bf16[128,1024]{1,0:T(8,128)(2,1)S(1)}, bf16[128,1024]{1,0:T(8,128)(2,1)S(1)}, u32[]{:S(2)}, u32[]{:S(2)}) collective-permute-start(bf16[128,1024]{1,0:T(8,128)(2,1)S(1)} %collective-permute-done), channel_id=1, source_target_pairs={{0,1},{1,2},{2,3},{3,4},{4,5},{5,6},{6,7},{7,0},{8,9},{9,10},{10,1... | collective-permute-start | bytes 786440 | tf_op jit(solution)/shard_map/ppermute | solution.py:23
  24.1 15.4 %copy-start.12 = (bf16[128,1024]{1,0:T(8,128)(2,1)}, bf16[128,1024]{1,0:T(8,128)(2,1)S(1)}, u32[]{:S(2)}) copy-start(bf16[128,1024]{1,0:T(8,128)(2,1)S(1)} %collective-permute-done.1) | copy-start | bytes 786436
  24.1 13.5 %collective-permute-start.2 = (bf16[128,1024]{1,0:T(8,128)(2,1)S(1)}, bf16[128,1024]{1,0:T(8,128)(2,1)}, u32[]{:S(2)}, u32[]{:S(2)}) collective-permute-start(bf16[128,1024]{1,0:T(8,128)(2,1)S(1)} %collective-permute-done.1), channel_id=1, source_target_pairs={{0,1},{1,2},{2,3},{3,4},{4,5},{5,6},{6,7},{7,0},{8,9},{9,10},{10,1... | collective-permute-start | bytes 786440 | tf_op jit(solution)/shard_map/ppermute | solution.py:23
  24.9 17.4 %collective-permute-start.5 = (bf16[128,1024]{1,0:T(8,128)(2,1)}, bf16[128,1024]{1,0:T(8,128)(2,1)}, u32[]{:S(2)}, u32[]{:S(2)}) collective-permute-start(bf16[128,1024]{1,0:T(8,128)(2,1)} %collective-permute-done.4), channel_id=1, source_target_pairs={{1,0},{2,1},{3,2},{4,3},{5,4},{6,5},{7,6},{0,7},{9,8},{10,9},{11,1... | collective-permute-start | bytes 786440 | tf_op jit(solution)/shard_map/ppermute | solution.py:25
  37.6 13.5 %collective-permute-start.3 = (bf16[128,1024]{1,0:T(8,128)(2,1)}, bf16[128,1024]{1,0:T(8,128)(2,1)}, u32[]{:S(2)}, u32[]{:S(2)}) collective-permute-start(bf16[128,1024]{1,0:T(8,128)(2,1)} %collective-permute-done.2), channel_id=1, source_target_pairs={{0,1},{1,2},{2,3},{3,4},{4,5},{5,6},{6,7},{7,0},{8,9},{9,10},{10,1... | collective-permute-start | bytes 786440 | tf_op jit(solution)/shard_map/ppermute | solution.py:23
  39.5 18.3 %copy-start.10 = (bf16[128,1024]{1,0:T(8,128)(2,1)S(1)}, bf16[128,1024]{1,0:T(8,128)(2,1)}, u32[]{:S(2)}) copy-start(bf16[128,1024]{1,0:T(8,128)(2,1)} %param.17) | copy-start | bytes 786436
  40.3 28.7 %copy-start.13 = (f32[8,4]{1,0:T(8,128)}, f32[8,4]{1,0:T(8,128)S(1)}, u32[]{:S(2)}) copy-start(f32[8,4]{1,0:T(8,128)S(1)} %broadcast_in_dim.234) | copy-start | bytes 388
  41.0 25.2 %copy-start.7 = (bf16[128,4096]{0,1:T(8,128)(2,1)}, bf16[128,4096]{0,1:T(8,128)(2,1)S(1)}, u32[]{:S(2)}) copy-start(bf16[128,4096]{0,1:T(8,128)(2,1)S(1)} %copy.98) | copy-start | bytes 3145732
  42.3 19.5 %collective-permute-start.6 = (bf16[128,1024]{1,0:T(8,128)(2,1)}, bf16[128,1024]{1,0:T(8,128)(2,1)S(1)}, u32[]{:S(2)}, u32[]{:S(2)}) collective-permute-start(bf16[128,1024]{1,0:T(8,128)(2,1)} %collective-permute-done.5), channel_id=1, source_target_pairs={{1,0},{2,1},{3,2},{4,3},{5,4},{6,5},{7,6},{0,7},{9,8},{10,9},{11,1... | collective-permute-start | bytes 786440 | tf_op jit(solution)/shard_map/ppermute | solution.py:25
  102.7 4.5 %copy-start.1 = (bf16[1024,1024]{0,1:T(8,128)(2,1)S(1)}, bf16[1024,1024]{0,1:T(8,128)(2,1)}, u32[]{:S(2)}) copy-start(bf16[1024,1024]{0,1:T(8,128)(2,1)} %get-tuple-element.1713) | copy-start | bytes 6291460 | tf_op jit(solution)/shard_map/while
  116.1 5.0 %copy-start = (f32[512,8,128]{2,0,1:T(8,128)S(1)}, f32[512,8,128]{2,0,1:T(8,128)}, u32[]{:S(2)}) copy-start(f32[512,8,128]{2,0,1:T(8,128)} %fusion.117) | copy-start | bytes 6291460 | tf_op jit(solution)/shard_map/while
  116.1 5.5 %copy-start.3 = (f32[1024,8,128]{2,1,0:T(8,128)S(1)}, f32[1024,8,128]{2,1,0:T(8,128)}, u32[]{:S(2)}) copy-start(f32[1024,8,128]{2,1,0:T(8,128)} %get-tuple-element.1685) | copy-start | bytes 12582916 | tf_op jit(solution)/shard_map/while
  116.1 6.7 %copy-start.5 = (f32[1024,8,128]{2,1,0:T(8,128)S(1)}, f32[1024,8,128]{2,1,0:T(8,128)}, u32[]{:S(2)}) copy-start(f32[1024,8,128]{2,1,0:T(8,128)} %get-tuple-element.1686) | copy-start | bytes 12582916 | tf_op jit(solution)/shard_map/while
  125.7 2.0 copy-start.4
  127.7 1.9 copy-start.6
  130.1 4.5 %copy-start.1 = (bf16[1024,1024]{0,1:T(8,128)(2,1)S(1)}, bf16[1024,1024]{0,1:T(8,128)(2,1)}, u32[]{:S(2)}) copy-start(bf16[1024,1024]{0,1:T(8,128)(2,1)} %get-tuple-element.1713) | copy-start | bytes 6291460 | tf_op jit(solution)/shard_map/while
  143.4 5.0 %copy-start = (f32[512,8,128]{2,0,1:T(8,128)S(1)}, f32[512,8,128]{2,0,1:T(8,128)}, u32[]{:S(2)}) copy-start(f32[512,8,128]{2,0,1:T(8,128)} %fusion.117) | copy-start | bytes 6291460 | tf_op jit(solution)/shard_map/while
  143.4 5.5 %copy-start.3 = (f32[1024,8,128]{2,1,0:T(8,128)S(1)}, f32[1024,8,128]{2,1,0:T(8,128)}, u32[]{:S(2)}) copy-start(f32[1024,8,128]{2,1,0:T(8,128)} %get-tuple-element.1685) | copy-start | bytes 12582916 | tf_op jit(solution)/shard_map/while
  143.4 6.7 %copy-start.5 = (f32[1024,8,128]{2,1,0:T(8,128)S(1)}, f32[1024,8,128]{2,1,0:T(8,128)}, u32[]{:S(2)}) copy-start(f32[1024,8,128]{2,1,0:T(8,128)} %get-tuple-element.1686) | copy-start | bytes 12582916 | tf_op jit(solution)/shard_map/while
  153.0 2.0 copy-start.4
  155.0 1.9 copy-start.6
  175.0 0.7 copy-start.14
  225.8 4.5 %copy-start.2 = (bf16[512,1024]{0,1:T(8,128)(2,1)}, bf16[512,1024]{0,1:T(8,128)(2,1)S(1)}, u32[]{:S(2)}) copy-start(bf16[512,1024]{0,1:T(8,128)(2,1)S(1)} %get-tuple-element.1529) | copy-start | bytes 3145732 | tf_op jit(solution)/shard_map/while
  242.7 4.5 %copy-start.2 = (bf16[512,1024]{0,1:T(8,128)(2,1)}, bf16[512,1024]{0,1:T(8,128)(2,1)S(1)}, u32[]{:S(2)}) copy-start(bf16[512,1024]{0,1:T(8,128)(2,1)S(1)} %get-tuple-element.1529) | copy-start | bytes 3145732 | tf_op jit(solution)/shard_map/while
  257.4 3.2 %copy-start.8 = (bf16[128,8,4,128]{0,3,2,1:T(8,128)(2,1)S(1)}, bf16[128,8,4,128]{0,3,2,1:T(8,128)(2,1)}, u32[]{:S(2)}) copy-start(bf16[128,8,4,128]{0,3,2,1:T(8,128)(2,1)} %get-tuple-element.1216) | copy-start | bytes 3145732
Sparse Core Ops, SparseCore 0:
  13.8 39.6 all-gather.1
  175.2 92.4 reduce-scatter.1
